TPU v7x, 32 devices: a whole 2x2x4 slice. The times are simulated.
32 devices in a mesh: fsdp: 4 (over z), ctx: 4 (over x, core), tp: 2 (over y).
Axes of the slice: x: 2, y: 2, z: 4, core: 2. Of those that a mesh axis runs over, the one named last changes fastest.
Arguments:
- layer_input: bfloat16 [4, 8, 512, 768], P(None, 'fsdp', 'ctx'), may hold values from -6 to 6
- doc_ids: int32 [4, 8, 512], P(None, 'fsdp', 'ctx'), may hold values from 0 to 3, never falling along the last dimension, each value on 1 to 256 neighbouring positions
- w_qkv: bfloat16 [3, 768, 768], P(None, 'fsdp', 'tp'), may hold values from -0.21875 to 0.21875
- b_qv: float32 [2, 768], P(None, 'tp'), may hold values from -3 to 3
- w_out: bfloat16 [768, 768], P('tp', 'fsdp'), may hold values from -0.625 to 0.625
- b_out: float32 [768], replicated, may hold values from -2 to 2
- ln1_gain: float32 [768], replicated, may hold values from 0.1 to 1.9
- ln1_bias: float32 [768], replicated, may hold values from -2 to 2
- w_up: bfloat16 [768, 3072], P('fsdp', 'tp'), may hold values from -0.21875 to 0.21875
- b_up: float32 [3072], P('tp'), may hold values from -3 to 3
- w_down: bfloat16 [3072, 768], P('tp', 'fsdp'), may hold values from -0.109375 to 0.109375
- b_down: float32 [768], replicated, may hold values from -2 to 2
- ln2_gain: float32 [768], replicated, may hold values from 0.1 to 1.9
- ln2_bias: float32 [768], replicated, may hold values from -2 to 2
- out_grad: bfloat16 [4, 8, 512, 768], P(None, 'fsdp', 'ctx'), may hold values from -6 to 6
Outputs:
- layer_output: bfloat16 [4, 8, 512, 768], P(None, 'fsdp', 'ctx')
- grad_x: bfloat16 [4, 8, 512, 768], P(None, 'fsdp', 'ctx')
- grad_w_qkv: float32 [3, 768, 768], P(None, 'fsdp', 'tp')
- grad_b_qv: float32 [2, 768], P(None, 'tp')
- grad_w_out: float32 [768, 768], P('tp', 'fsdp')
- grad_b_out: float32 [768], replicated
- grad_ln1_gain: float32 [768], replicated
- grad_ln1_bias: float32 [768], replicated
- grad_w_up: float32 [768, 3072], P('fsdp', 'tp')
- grad_b_up: float32 [3072], P('tp')
- grad_w_down: float32 [3072, 768], P('tp', 'fsdp')
- grad_b_down: float32 [768], replicated
- grad_ln2_gain: float32 [768], replicated
- grad_ln2_bias: float32 [768], replicated
Inputs may be any that keep to these rules, and one draw needn't show every extreme that they name: `doc_ids`: within each sequence of 512 tokens the ids never fall and each of the 4 ids marks one run of 1 to 256 tokens.
All inputs are finite; a program needn't handle non-finite values.
Results may differ from a plain program's by a relative error of at most 0.02.
Values may be sent and summed in bfloat16 or wider, within the bound.
No kernel may reach another device: no remote copies, remote signals or barrier semaphores. Data moves between devices by JAX's collectives and lax.ppermute only.
A program may use at most 128 MiB of HBM per device.

v0:
```python
import jax
import jax.numpy as jnp
from jax import lax
from jax.sharding import PartitionSpec as P

HEAD_DIM = 64


def normalize_rows(values_in):
    mean = jnp.mean(values_in, axis=-1, keepdims=True)
    centred = values_in - mean
    var = jnp.mean(centred * centred, axis=-1, keepdims=True)
    scale = lax.rsqrt(var + 1e-12)
    return (centred * scale, scale)


def normalize_back(grad_hat, normed, scale):
    first_mean = jnp.mean(grad_hat, axis=-1, keepdims=True)
    second_mean = jnp.mean(grad_hat * normed, axis=-1, keepdims=True)
    return scale * (grad_hat - first_mean - normed * second_mean)


def collect_weights(weights):
    return (
        lax.all_gather(weights[0], "fsdp", axis=1, tiled=True),
        lax.all_gather(weights[1], "fsdp", axis=1, tiled=True),
        lax.all_gather(weights[2], "fsdp", axis=0, tiled=True),
        lax.all_gather(weights[3], "fsdp", axis=1, tiled=True),
    )


def spread_grads(grads):
    return (
        lax.psum_scatter(
            grads[0].astype(jnp.bfloat16), "fsdp", scatter_dimension=1, tiled=True
        ).astype(jnp.float32),
        lax.psum_scatter(
            grads[1].astype(jnp.bfloat16), "fsdp", scatter_dimension=1, tiled=True
        ).astype(jnp.float32),
        lax.psum_scatter(
            grads[2].astype(jnp.bfloat16), "fsdp", scatter_dimension=0, tiled=True
        ).astype(jnp.float32),
        lax.psum_scatter(
            grads[3].astype(jnp.bfloat16), "fsdp", scatter_dimension=1, tiled=True
        ).astype(jnp.float32),
    )


def attention_probs(query, keys, allowed, log_total):
    scores = jnp.einsum("sqhd,skhd->shqk", query, keys, preferred_element_type=jnp.float32) * 0.125
    masked = jnp.where(allowed, scores, -1e30)
    if log_total is None:
        top = jnp.max(masked, axis=-1, keepdims=True)
        log_total = top + jnp.log(jnp.sum(jnp.exp(masked - top), axis=-1, keepdims=True))
    return (jnp.exp(masked - log_total), log_total)


def body(
    layer_input,
    doc_ids,
    w_qkv,
    b_qv,
    w_out,
    b_out,
    ln1_gain,
    ln1_bias,
    w_up,
    b_up,
    w_down,
    b_down,
    ln2_gain,
    ln2_bias,
    out_grad,
):
    inputs_here, cot_here, ids_here = (layer_input, out_grad, doc_ids)
    key_ids = lax.all_gather(doc_ids, "ctx", axis=2, tiled=True)
    micro, seqs, local_len, width = inputs_here.shape
    full_len = key_ids.shape[2]
    shard_rows = width // lax.axis_size("fsdp")
    local_width = w_qkv.shape[2]
    local_units = w_up.shape[1]
    local_heads = local_width // HEAD_DIM
    rows_count = seqs * local_len
    bias_three = jnp.concatenate(
        [b_qv[0:1], jnp.zeros((1, local_width), jnp.float32), b_qv[1:2]], axis=0
    )[:, None, :]
    local_acc = (
        jnp.zeros((3, width, local_width), jnp.float32),
        jnp.zeros((local_width, width), jnp.float32),
        jnp.zeros((width, local_units), jnp.float32),
        jnp.zeros((local_units, width), jnp.float32),
    )
    shard_acc = (
        jnp.zeros((3, shard_rows, local_width), jnp.float32),
        jnp.zeros((local_width, shard_rows), jnp.float32),
        jnp.zeros((shard_rows, local_units), jnp.float32),
        jnp.zeros((local_units, shard_rows), jnp.float32),
    )
    zero_width = jnp.zeros((width,), jnp.float32)
    grad_bqv = jnp.zeros((2, local_width), jnp.float32)
    grad_bup = jnp.zeros((local_units,), jnp.float32)
    grad_bout, grad_gain1, grad_shift1 = (zero_width, zero_width, zero_width)
    grad_bdown, grad_gain2, grad_shift2 = (zero_width, zero_width, zero_width)
    outputs, input_grads = ([], [])
    for micro_step in range(micro):
        weights_now = collect_weights((w_qkv, w_out, w_up, w_down))
        wq_all, wo_all, wu_all, wd_all = weights_now
        rows_b = inputs_here[micro_step].reshape(rows_count, width)
        rows_f = rows_b.astype(jnp.float32)
        projected = (
            jnp.einsum("rd,cde->cre", rows_b, wq_all, preferred_element_type=jnp.float32)
            + bias_three
        )
        proj_b = projected.astype(jnp.bfloat16)
        query = proj_b[0].reshape(seqs, local_len, local_heads, HEAD_DIM)
        local_kv = proj_b[1:].reshape(2, seqs, local_len, local_width)
        full_kv = lax.all_gather(local_kv, "ctx", axis=2, tiled=True)
        keys = full_kv[0].reshape(seqs, full_len, local_heads, HEAD_DIM)
        values = full_kv[1].reshape(seqs, full_len, local_heads, HEAD_DIM)
        allowed = ids_here[micro_step][:, None, :, None] == key_ids[micro_step][:, None, None, :]
        probs, log_total = attention_probs(query, keys, allowed, None)
        probs_b = probs.astype(jnp.bfloat16)
        mixed = jnp.einsum("shqk,skhd->sqhd", probs_b, values, preferred_element_type=jnp.float32)
        mixed_b = mixed.reshape(rows_count, local_width).astype(jnp.bfloat16)
        branch = lax.psum(jnp.dot(mixed_b, wo_all, preferred_element_type=jnp.float32), "tp")
        normed1, scale1 = normalize_rows(rows_f + branch + b_out)
        first = normed1 * ln1_gain + ln1_bias
        first_b = first.astype(jnp.bfloat16)
        hidden = jnp.dot(first_b, wu_all, preferred_element_type=jnp.float32) + b_up
        activation, gelu_pull = jax.vjp(
            lambda hidden_in: jax.nn.gelu(hidden_in, approximate=False), hidden
        )
        act_b = activation.astype(jnp.bfloat16)
        second = lax.psum(
            jnp.dot(act_b, wd_all, preferred_element_type=jnp.float32).astype(jnp.bfloat16), "tp"
        ).astype(jnp.float32)
        normed2, scale2 = normalize_rows(first + second + b_down)
        result = normed2 * ln2_gain + ln2_bias
        outputs.append(result.astype(jnp.bfloat16).reshape(seqs, local_len, width))
        incoming = cot_here[micro_step].reshape(rows_count, width).astype(jnp.float32)
        grad_gain2 = grad_gain2 + jnp.sum(incoming * normed2, axis=0)
        grad_shift2 = grad_shift2 + jnp.sum(incoming, axis=0)
        grad_z2 = normalize_back(incoming * ln2_gain, normed2, scale2)
        grad_bdown = grad_bdown + jnp.sum(grad_z2, axis=0)
        grad_second_b = grad_z2.astype(jnp.bfloat16)
        step_wd = jnp.dot(act_b.T, grad_second_b, preferred_element_type=jnp.float32)
        grad_act = jnp.dot(grad_second_b, wd_all.T, preferred_element_type=jnp.float32)
        (grad_hidden,) = gelu_pull(grad_act)
        grad_hidden_b = grad_hidden.astype(jnp.bfloat16)
        grad_bup = grad_bup + jnp.sum(grad_hidden_b.astype(jnp.float32), axis=0)
        step_wu = jnp.dot(first_b.T, grad_hidden_b, preferred_element_type=jnp.float32)
        grad_first = grad_z2 + lax.psum(
            jnp.dot(grad_hidden_b, wu_all.T, preferred_element_type=jnp.float32).astype(
                jnp.bfloat16
            ),
            "tp",
        ).astype(jnp.float32)
        grad_gain1 = grad_gain1 + jnp.sum(grad_first * normed1, axis=0)
        grad_shift1 = grad_shift1 + jnp.sum(grad_first, axis=0)
        grad_z1 = normalize_back(grad_first * ln1_gain, normed1, scale1)
        grad_bout = grad_bout + jnp.sum(grad_z1, axis=0)
        grad_branch_b = grad_z1.astype(jnp.bfloat16)
        step_wo = jnp.dot(mixed_b.T, grad_branch_b, preferred_element_type=jnp.float32)
        grad_mixed_b = jnp.dot(grad_branch_b, wo_all.T, preferred_element_type=jnp.float32).astype(
            jnp.bfloat16
        )
        grad_mixed_b = grad_mixed_b.reshape(seqs, local_len, local_heads, HEAD_DIM)
        recomputed, unused_total = attention_probs(query, keys, allowed, log_total)
        recomputed_b = recomputed.astype(jnp.bfloat16)
        grad_probs = jnp.einsum(
            "sqhd,skhd->shqk", grad_mixed_b, values, preferred_element_type=jnp.float32
        )
        weighted = jnp.sum(recomputed * grad_probs, axis=-1, keepdims=True)
        grad_scores_b = (recomputed * (grad_probs - weighted)).astype(jnp.bfloat16)
        grad_query = (
            jnp.einsum("shqk,skhd->sqhd", grad_scores_b, keys, preferred_element_type=jnp.float32)
            * 0.125
        )
        grad_keys = (
            jnp.einsum("shqk,sqhd->skhd", grad_scores_b, query, preferred_element_type=jnp.float32)
            * 0.125
        )
        grad_values = jnp.einsum(
            "shqk,sqhd->skhd", recomputed_b, grad_mixed_b, preferred_element_type=jnp.float32
        )
        kv_terms = jnp.stack([grad_keys, grad_values]).reshape(2, seqs, full_len, local_width)
        kv_back = lax.psum_scatter(
            kv_terms.astype(jnp.bfloat16), "ctx", scatter_dimension=2, tiled=True
        ).astype(jnp.float32)
        grad_proj_b = jnp.concatenate(
            [
                grad_query.reshape(1, rows_count, local_width).astype(jnp.bfloat16),
                kv_back.reshape(2, rows_count, local_width).astype(jnp.bfloat16),
            ],
            axis=0,
        )
        grad_bqv = grad_bqv + jnp.sum(grad_proj_b[0::2].astype(jnp.float32), axis=1)
        step_wq = jnp.einsum("rd,cre->cde", rows_b, grad_proj_b, preferred_element_type=jnp.float32)
        back_rows = jnp.einsum(
            "cre,cde->rd", grad_proj_b, wq_all, preferred_element_type=jnp.float32
        )
        grad_rows = grad_z1 + lax.psum(back_rows.astype(jnp.bfloat16), "tp").astype(jnp.float32)
        input_grads.append(grad_rows.astype(jnp.bfloat16).reshape(seqs, local_len, width))
        step_grads = (step_wq, step_wo, step_wu, step_wd)
        local_acc = tuple((left + right for left, right in zip(local_acc, step_grads)))
    shard_acc = spread_grads(local_acc)
    small_sums = lax.psum(
        (
            grad_bqv,
            grad_bout,
            grad_gain1,
            grad_shift1,
            grad_bup,
            grad_bdown,
            grad_gain2,
            grad_shift2,
        ),
        "fsdp",
    )
    summed = (
        lax.psum(shard_acc[0].astype(jnp.bfloat16), "ctx").astype(jnp.float32),
        lax.psum(shard_acc[1].astype(jnp.bfloat16), "ctx").astype(jnp.float32),
        lax.psum(shard_acc[2].astype(jnp.bfloat16), "ctx").astype(jnp.float32),
        lax.psum(shard_acc[3].astype(jnp.bfloat16), "ctx").astype(jnp.float32),
        lax.psum(small_sums[0].astype(jnp.bfloat16), "ctx").astype(jnp.float32),
        lax.psum(small_sums[1].astype(jnp.bfloat16), "ctx").astype(jnp.float32),
        lax.psum(small_sums[2].astype(jnp.bfloat16), "ctx").astype(jnp.float32),
        lax.psum(small_sums[3].astype(jnp.bfloat16), "ctx").astype(jnp.float32),
        lax.psum(small_sums[4].astype(jnp.bfloat16), "ctx").astype(jnp.float32),
        lax.psum(small_sums[5].astype(jnp.bfloat16), "ctx").astype(jnp.float32),
        lax.psum(small_sums[6].astype(jnp.bfloat16), "ctx").astype(jnp.float32),
        lax.psum(small_sums[7].astype(jnp.bfloat16), "ctx").astype(jnp.float32),
    )
    stacked_out = jnp.stack(outputs)
    stacked_grad = jnp.stack(input_grads)
    return (
        stacked_out,
        stacked_grad,
        summed[0],
        summed[4],
        summed[1],
        summed[5],
        summed[6],
        summed[7],
        summed[2],
        summed[8],
        summed[3],
        summed[9],
        summed[10],
        summed[11],
    )


def solution(mesh):
    return jax.shard_map(
        body,
        mesh=mesh,
        in_specs=(
            P(None, "fsdp", "ctx", None),
            P(None, "fsdp", "ctx"),
            P(None, "fsdp", "tp"),
            P(None, "tp"),
            P("tp", "fsdp"),
            P(),
            P(),
            P(),
            P("fsdp", "tp"),
            P("tp"),
            P("tp", "fsdp"),
            P(),
            P(),
            P(),
            P(None, "fsdp", "ctx", None),
        ),
        out_specs=(
            P(None, "fsdp", "ctx", None),
            P(None, "fsdp", "ctx", None),
            P(None, "fsdp", "tp"),
            P(None, "tp"),
            P("tp", "fsdp"),
            P(),
            P(),
            P(),
            P("fsdp", "tp"),
            P("tp"),
            P("tp", "fsdp"),
            P(),
            P(),
            P(),
        ),
        check_vma=False,
    )
```

profile of v0, /device:TPU:0, one launch (start us, length us, event | category | flops | bytes accessed | tf_op | source)
XLA Modules:
  0.0 957.4 jit_solution(15539514754937439668)
XLA Ops:
  10.4 42.3 %all-gather.8.cloned.1.call-done = bf16[3,768,384]{2,1,0:T(8,128)(2,1)} async-done(((bf16[3,192,384]{2,1,0:T(8,128)(2,1)}), bf16[3,768,384]{2,1,0:T(8,128)(2,1)}) %all-gather.8.cloned.1.call-update) | async-done | bytes 1769488 | tf_op jit(solution)/shard_map/all_gather | solution.py:25
  65.2 5.2 all_gather.20
  70.3 17.5 %all_gather.42 = bf16[384,768]{0,1:T(8,128)(2,1)} all-gather(bf16[384,192]{0,1:T(8,128)(2,1)S(1)} %copy-done.144), channel_id=1, replica_groups=mesh['fsdp'=4,'ctx'=4,'tp'=2] {'fsdp'}, dimensions={1}, use_global_device_ids=true | all-gather | bytes 737280 | tf_op jit(solution)/shard_map/all_gather | solution.py:26
  98.8 18.0 %all-gather.20.cloned.1.call-done = bf16[2,2,512,384]{3,2,1,0:T(8,128)(2,1)} async-done(((bf16[2,2,128,384]{3,2,1,0:T(8,128)(2,1)}), bf16[2,2,512,384]{3,2,1,0:T(8,128)(2,1)}) %all-gather.20.cloned.1.call-update) | async-done | bytes 1572880 | tf_op jit(solution)/shard_map/all_gather | solution.py:117
  119.5 19.0 %all-gather.18.cloned.1.call-done = bf16[2,2,512,384]{3,2,1,0:T(8,128)(2,1)} async-done(((bf16[2,2,128,384]{3,2,1,0:T(8,128)(2,1)}), bf16[2,2,512,384]{3,2,1,0:T(8,128)(2,1)}) %all-gather.18.cloned.1.call-update) | async-done | bytes 1572880 | tf_op jit(solution)/shard_map/all_gather | solution.py:117
  171.0 84.9 %all-reduce.13.cloned.1.call-done = (f32[256,768]{1,0:T(8,128)}, f32[256,768]{1,0:T(8,128)}, f32[256,768]{1,0:T(8,128)}, f32[256,768]{1,0:T(8,128)}) async-done(((f32[256,768]{1,0:T(8,128)}, f32[256,768]{1,0:T(8,128)}, f32[256,768]{1,0:T(8,128)}, f32[256,768]{1,0:T(8,128)}), (f32[256,768]{1,0:T(8,128)}, f32[256,768]{1,0:T(8,128)}, f32[256,768]{1,0:T(8,128)}, ...) | async-done | bytes 3145744 | tf_op jit(solution)/shard_map/psum | solution.py:125
  262.6 45.5 %all-gather.12.cloned.1.call-done = bf16[768,1536]{1,0:T(8,128)(2,1)} async-done(((bf16[192,1536]{1,0:T(8,128)(2,1)}), bf16[768,1536]{1,0:T(8,128)(2,1)}) %all-gather.12.cloned.1.call-update) | async-done | bytes 2359312 | tf_op jit(solution)/shard_map/all_gather | solution.py:27
  308.1 7.9 multiply_convert_fusion.10
  316.1 5.8 multiply_convert_fusion.9
  321.8 37.2 %all-gather.14.cloned.1.call-done = bf16[1536,768]{0,1:T(8,128)(2,1)} async-done(((bf16[1536,192]{0,1:T(8,128)(2,1)}), bf16[1536,768]{0,1:T(8,128)(2,1)}) %all-gather.14.cloned.1.call-update) | async-done | bytes 2359312 | tf_op jit(solution)/shard_map/all_gather | solution.py:28
  364.8 5.2 multiply_convert_fusion.8
  372.5 5.2 multiply_convert_fusion.11
  384.0 47.1 %all-reduce.21.cloned.1.call-done = (bf16[256,768]{1,0:T(8,128)(2,1)}, bf16[256,768]{1,0:T(8,128)(2,1)}, bf16[256,768]{1,0:T(8,128)(2,1)}, bf16[256,768]{1,0:T(8,128)(2,1)}) async-done(((bf16[256,768]{1,0:T(8,128)(2,1)}, bf16[256,768]{1,0:T(8,128)(2,1)}, bf16[256,768]{1,0:T(8,128)(2,1)}, bf16[256,768]{1,0:T(8,128)(2,1)}), (bf16[256,768]{1,0:T(8,128)(2,1)}, bf16[256,768]{1,0:T(8,128)(2,1)}, ...) | async-done | bytes 1572880 | tf_op jit(solution)/shard_map/psum | solution.py:134
  461.9 52.0 %all-reduce.19.cloned.1.call-done = (bf16[256,768]{1,0:T(8,128)(2,1)}, bf16[256,768]{1,0:T(8,128)(2,1)}, bf16[256,768]{1,0:T(8,128)(2,1)}, bf16[256,768]{1,0:T(8,128)(2,1)}) async-done(((bf16[256,768]{1,0:T(8,128)(2,1)}, bf16[256,768]{1,0:T(8,128)(2,1)}, bf16[256,768]{1,0:T(8,128)(2,1)}, bf16[256,768]{1,0:T(8,128)(2,1)}), (bf16[256,768]{1,0:T(8,128)(2,1)}, bf16[256,768]{1,0:T(8,128)(2,1)}, ...) | async-done | bytes 1572880 | tf_op jit(solution)/shard_map/psum | solution.py:152
  562.5 5.0 copy.174
  630.6 7.0 reduce-scatter.25.cloned.1.call-done
  638.8 30.0 %reduce-scatter.29.cloned.1.call-done = bf16[128,1536]{1,0:T(8,128)(2,1)} async-done(((bf16[512,1536]{1,0:T(8,128)(2,1)}), bf16[128,1536]{1,0:T(8,128)(2,1)}) %reduce-scatter.29.cloned.1.call-update) | async-done | bytes 393232
  717.7 19.4 %all-reduce = (bf16[2,384]{1,0:T(2,128)(2,1)S(1)}, bf16[768]{0:T(1024)(128)(2,1)S(1)}, bf16[768]{0:T(1024)(128)(2,1)S(1)}, bf16[768]{0:T(1024)(128)(2,1)S(1)}, b...) all-reduce(f32[2,384]{1,0:T(2,128)S(1)} %add_add_fusion.15, ...), channel_id=1, replica_groups=mesh['fsdp'=4,'ctx'=4,'tp'=2] {'fsdp'}, use_global_device_ids=true, to_apply=%region_70.71 | all-reduce | flops 6912 | bytes 41472 | tf_op jit(solution)/shard_map/psum | solution.py:207
  737.0 11.0 %all-reduce.2 = (bf16[2,384]{1,0:T(2,128)(2,1)S(1)}, bf16[768]{0:T(1024)(128)(2,1)S(1)}, bf16[768]{0:T(1024)(128)(2,1)S(1)}, bf16[768]{0:T(1024)(128)(2,1)S(1)},...) all-reduce(bf16[2,384]{1,0:T(2,128)(2,1)S(1)} %get-tuple-element.10, ...), channel_id=1, replica_groups=mesh['fsdp'=4,'ctx'=4,'tp'=2] {'ctx'}, use_global_device_ids=true, to_apply=%region_71.72 | all-reduce | flops 6912 | bytes 27648 | tf_op jit(solution)/shard_map/psum | solution.py:225
  753.9 16.5 %reduce-scatter.33.cloned.1.call-done = bf16[192,1152]{1,0:T(8,128)(2,1)} async-done(((bf16[768,1152]{1,0:T(8,128)(2,1)}), bf16[192,1152]{1,0:T(8,128)(2,1)}) %reduce-scatter.33.cloned.1.call-update) | async-done | bytes 442384
  773.1 21.2 %reduce-scatter.19.cloned.1.call-done = bf16[384,192]{0,1:T(8,128)(2,1)} async-done(((bf16[384,768]{0,1:T(8,128)(2,1)}), bf16[384,192]{0,1:T(8,128)(2,1)}) %reduce-scatter.19.cloned.1.call-update) | async-done | bytes 147472 | tf_op jit(solution)/shard_map/reduce_scatter | solution.py:37
  794.3 48.7 %reduce-scatter.21.cloned.1.call-done = bf16[192,1536]{1,0:T(8,128)(2,1)} async-done(((bf16[768,1536]{1,0:T(8,128)(2,1)}), bf16[192,1536]{1,0:T(8,128)(2,1)}) %reduce-scatter.21.cloned.1.call-update) | async-done | bytes 589840 | tf_op jit(solution)/shard_map/reduce_scatter | solution.py:40
  843.0 50.0 %reduce-scatter.23.cloned.1.call-done = bf16[1536,192]{0,1:T(8,128)(2,1)} async-done(((bf16[1536,768]{0,1:T(8,128)(2,1)}), bf16[1536,192]{0,1:T(8,128)(2,1)}) %reduce-scatter.23.cloned.1.call-update) | async-done | bytes 589840 | tf_op jit(solution)/shard_map/reduce_scatter | solution.py:43
  895.7 49.2 %all-reduce.15.cloned.1.call-done = (bf16[3,192,384]{1,2,0:T(8,128)(2,1)}, bf16[384,192]{0,1:T(8,128)(2,1)}, bf16[192,1536]{1,0:T(8,128)(2,1)}, bf16[1536,192]{0,1:T(8,128)(2,1)}) async-done(((bf16[3,192,384]{1,2,0:T(8,128)(2,1)}, bf16[384,192]{0,1:T(8,128)(2,1)}, bf16[192,1536]{1,0:T(8,128)(2,1)}, bf16[1536,192]{0,1:T(8,128)(2,1)}), (bf16[3,192,384]{1,2,0:T(8,128)(2,1)}, bf16[384,192]{0,1:T(8,128)(2,1)}, ...) | async-done | bytes 1769488 | tf_op jit(solution)/shard_map/psum | solution.py:221
  (771 shorter events, 289.2 us)
Async XLA Ops:
  7.2 45.5 %all-gather.8.cloned.1.call-start = ((), (), s32[]{:S(2)}) async-start(), calls=%async_computation.8 | async-start | bytes 2211840 | tf_op jit(solution)/shard_map/all_gather | solution.py:25
  7.9 85.4 %all-gather.10.cloned.1.call-start = ((), (), s32[]{:S(2)}) async-start(), calls=%async_computation.9 | async-start | bytes 1966080 | tf_op jit(solution)/shard_map/all_gather | solution.py:117
  10.4 51.5 %copy-start.62 = (bf16[1,2,128,768]{3,2,1,0:T(8,128)(2,1)}, bf16[1,2,128,768]{3,2,1,0:T(8,128)(2,1)S(1)}, u32[]{:S(2)}) copy-start(bf16[1,2,128,768]{3,2,1,0:T(8,128)(2,1)S(1)} %get-tuple-element.177) | copy-start | bytes 1179652
  55.6 40.4 %all-gather.16.cloned.1.call-start = ((), (), s32[]{:S(2)}) async-start(), calls=%async_computation.12 | async-start | bytes 1966080 | tf_op jit(solution)/shard_map/all_gather | solution.py:117
  58.7 58.0 %all-gather.20.cloned.1.call-start = ((), (), s32[]{:S(2)}) async-start(), calls=%async_computation.14 | async-start | bytes 1966080 | tf_op jit(solution)/shard_map/all_gather | solution.py:117
  61.8 76.6 %all-gather.18.cloned.1.call-start = ((), (), s32[]{:S(2)}) async-start(), calls=%async_computation.13 | async-start | bytes 1966080 | tf_op jit(solution)/shard_map/all_gather | solution.py:117
  65.1 190.8 %all-reduce.13.cloned.1.call-start = ((), (), s32[]{:S(2)}) async-start(), calls=%async_computation.23 | async-start | bytes 6291456 | tf_op jit(solution)/shard_map/psum | solution.py:125
  169.4 86.5 %copy-start.215 = (f32[768]{0:T(1024)S(1)}, f32[768]{0:T(1024)}, u32[]{:S(2)}) copy-start(f32[768]{0:T(1024)} %param.20) | copy-start | bytes 9220
  169.4 138.7 %all-gather.12.cloned.1.call-start = ((), (), s32[]{:S(2)}) async-start(), calls=%async_computation.10 | async-start | bytes 2949120 | tf_op jit(solution)/shard_map/all_gather | solution.py:27
  170.2 188.9 %all-gather.14.cloned.1.call-start = ((), (), s32[]{:S(2)}) async-start(), calls=%async_computation.11 | async-start | bytes 2949120 | tf_op jit(solution)/shard_map/all_gather | solution.py:28
  170.9 260.2 %all-reduce.21.cloned.1.call-start = ((), (), s32[]{:S(2)}) async-start(), calls=%async_computation.27 | async-start | bytes 3145728 | tf_op jit(solution)/shard_map/psum | solution.py:134
  380.2 133.7 %all-reduce.19.cloned.1.call-start = ((), (), s32[]{:S(2)}) async-start(), calls=%async_computation.26 | async-start | bytes 3145728 | tf_op jit(solution)/shard_map/psum | solution.py:152
  461.6 166.4 %reduce-scatter.31.cloned.1.call-start = ((), (), s32[]{:S(2)}) async-start(), calls=%async_computation.21 | async-start | bytes 1966080
  547.8 81.5 %reduce-scatter.27.cloned.1.call-start = ((), (), s32[]{:S(2)}) async-start(), calls=%async_computation.19 | async-start | bytes 1966080
  572.4 65.2 %reduce-scatter.25.cloned.1.call-start = ((), (), s32[]{:S(2)}) async-start(), calls=%async_computation.18 | async-start | bytes 1966080
  596.2 72.6 %reduce-scatter.29.cloned.1.call-start = ((), (), s32[]{:S(2)}) async-start(), calls=%async_computation.20 | async-start | bytes 1966080
  615.6 137.2 %all-reduce.17.cloned.1.call-start = ((), (), s32[]{:S(2)}) async-start(), calls=%async_computation.25 | async-start | bytes 3145728 | tf_op jit(solution)/shard_map/psum | solution.py:202
  629.3 51.7 %copy-start.64 = (bf16[2,2,128,384]{3,2,1,0:T(8,128)(2,1)}, bf16[2,2,128,384]{3,2,1,0:T(8,128)(2,1)S(1)}, u32[]{:S(2)}) copy-start(bf16[2,2,128,384]{3,2,1,0:T(8,128)(2,1)S(1)} %copy.161) | copy-start | bytes 1179652
  677.6 92.8 %reduce-scatter.33.cloned.1.call-start = ((), (), s32[]{:S(2)}) async-start(), calls=%async_computation.22 | async-start | bytes 2211840
  688.5 105.8 %reduce-scatter.19.cloned.1.call-start = ((), (), s32[]{:S(2)}) async-start(), calls=%async_computation.15 | async-start | bytes 737280 | tf_op jit(solution)/shard_map/reduce_scatter | solution.py:37
  697.8 145.2 %reduce-scatter.21.cloned.1.call-start = ((), (), s32[]{:S(2)}) async-start(), calls=%async_computation.16 | async-start | bytes 2949120 | tf_op jit(solution)/shard_map/reduce_scatter | solution.py:40
  704.3 188.6 %reduce-scatter.23.cloned.1.call-start = ((), (), s32[]{:S(2)}) async-start(), calls=%async_computation.17 | async-start | bytes 2949120 | tf_op jit(solution)/shard_map/reduce_scatter | solution.py:43
  712.9 232.0 %all-reduce.15.cloned.1.call-start = ((), (), s32[]{:S(2)}) async-start(), calls=%async_computation.24 | async-start | bytes 3833856 | tf_op jit(solution)/shard_map/psum | solution.py:221
  771.8 121.2 %copy-start.142 = (bf16[256,768]{1,0:T(8,128)(2,1)S(1)}, bf16[256,768]{1,0:T(8,128)(2,1)}, u32[]{:S(2)}) copy-start(bf16[256,768]{1,0:T(8,128)(2,1)} %get-tuple-element.126) | copy-start | bytes 1179652
  (237 other events, 1068.7 us)
Sparse Core Ops, SparseCore 0:
  9.6 43.0 all-gather.7
  55.7 18.6 all-gather.9
  76.0 19.6 all-gather.15
  97.1 19.6 all-gather.19
  118.7 19.6 all-gather.17
  169.6 86.3 all-reduce.12
  257.6 50.4 all-gather.11
  309.7 49.2 all-gather.13
  380.3 50.8 all-reduce.20
  461.8 52.0 all-reduce.18
  547.9 28.1 reduce-scatter.30
  578.5 28.1 reduce-scatter.26
  609.4 28.1 reduce-scatter.24
  640.6 28.1 reduce-scatter.28
  677.7 52.0 all-reduce.16
  732.0 38.3 reduce-scatter.32
  773.2 21.0 reduce-scatter.18
  796.6 46.3 reduce-scatter.20
  845.4 47.5 reduce-scatter.22
  896.2 48.6 all-reduce.14
where the time goes:
time: 963 us; the launch traced here: 957 us
  waiting for transfers between devices  571 us (59%)
  matrix products  130 us (13%)
  local copies, waits for them, and re-layouts  124 us (13%)
  other arithmetic  59.6 us (6%)
  blocking collectives  53.1 us (6%)
  between operations  17.5 us (2%)
    psum x1, waiting for transfers between devices, body(): lax.psum(jnp.dot(mixed_b, wo_all, preferred_element_type=jnp.float32), 'tp')  84.9 us
    unnamed x493, local copies, waits for them, and re-layouts  79.3 us
    unnamed x25, waiting for transfers between devices  55.9 us
    psum x1, waiting for transfers between devices, body(): lax.psum(jnp.dot(grad_hidden_b, wu_all.T, preferred_element_type=jnp.floa...  52 us
    reduce_scatter x1, waiting for transfers between devices, spread_grads(): lax.psum_scatter(grads[3].astype(jnp.bfloat16), 'fsdp', scatter_dimension...  50 us
    psum x1, waiting for transfers between devices, body(): lax.psum(shard_acc[0].astype(jnp.bfloat16), 'ctx').astype(jnp.float32)  49.2 us
    reduce_scatter x1, waiting for transfers between devices, spread_grads(): lax.psum_scatter(grads[2].astype(jnp.bfloat16), 'fsdp', scatter_dimension...  48.7 us
    psum x1, waiting for transfers between devices, body(): lax.psum(jnp.dot(act_b, wd_all, preferred_element_type=jnp.float32).astyp...  47.1 us
  transfers between devices with their start and end apart: 20, of which 15 were waited for; matrix products, arithmetic and copies ran while one was open for 17% of the time, Pallas kernels for 0%

commit v1 on v0

--- a/solution.py
+++ b/solution.py
@@ -4,6 +4,23 @@
 from jax.sharding import PartitionSpec as P
 
 HEAD_DIM = 64
+
+
+def joined_along(pieces, dim):
+    dims = list(pieces.shape[1:])
+    dims[dim] *= pieces.shape[0]
+    return jnp.moveaxis(pieces, 0, dim).reshape(dims)
+
+
+def collect(value, axis, dim):
+    length = lax.axis_size(axis)
+    right = [(i, (i + 1) % length) for i in range(length)]
+    pieces = [value]
+    while len(pieces) < length:
+        pieces.append(lax.ppermute(pieces[-1], axis, right))
+    position = lax.axis_index(axis)
+    pieces = jnp.stack(pieces)[(position - jnp.arange(length)) % length]
+    return joined_along(pieces, dim)
 
 
 def normalize_rows(values_in):
@@ -24,7 +41,7 @@
     return (
         lax.all_gather(weights[0], "fsdp", axis=1, tiled=True),
         lax.all_gather(weights[1], "fsdp", axis=1, tiled=True),
-        lax.all_gather(weights[2], "fsdp", axis=0, tiled=True),
+        collect(weights[2], "fsdp", 0),
         lax.all_gather(weights[3], "fsdp", axis=1, tiled=True),
     )
 

time: 963 us -> 899 us (0.934)
  waiting for transfers between devices: 571 us -> 503 us
    psum x1, waiting for transfers between devices: 84.9 us -> 28.3 us  [body(): lax.psum(jnp.dot(mixed_b, wo_all, preferred_element_type=jnp.float32), 'tp')]
    ppermute x0 -> x3, waiting for transfers between devices: none -> 48.3 us  [collect(): pieces.append(lax.ppermute(pieces[-1], axis, right))]
    all_gather x1 -> x0, waiting for transfers between devices: 45.5 us -> none  [collect_weights(): lax.all_gather(weights[2], 'fsdp', axis=0, tiled=True)]
    all_gather x1, waiting for transfers between devices: 37.2 us -> 24.6 us  [collect_weights(): lax.all_gather(weights[3], 'fsdp', axis=1, tiled=True)]
    unnamed x25 -> x24, waiting for transfers between devices: 55.9 us -> 54.7 us
    unnamed x493 -> x481, local copies, waits for them, and re-layouts: 79.3 us -> 78.9 us
  transfers between devices with their start and end apart: 20 -> 22, of which waited for: 15 -> 17; matrix products, arithmetic and copies ran while one was open for 17% -> 20% of each run, Pallas kernels for 0% -> 0%
where the time goes in v1:
time: 899 us; the launch traced here: 894 us
  waiting for transfers between devices  503 us (56%)
  matrix products  128 us (14%)
  local copies, waits for them, and re-layouts  127 us (14%)
  other arithmetic  61.1 us (7%)
  blocking collectives  53.1 us (6%)
  between operations  17.2 us (2%)
    unnamed x481, local copies, waits for them, and re-layouts  78.9 us
    unnamed x24, waiting for transfers between devices  54.7 us
    psum x1, waiting for transfers between devices, body(): lax.psum(jnp.dot(grad_hidden_b, wu_all.T, preferred_element_type=jnp.floa...  51.9 us
    reduce_scatter x1, waiting for transfers between devices, spread_grads(): lax.psum_scatter(grads[3].astype(jnp.bfloat16), 'fsdp', scatter_dimension...  49.8 us
    psum x1, waiting for transfers between devices, body(): lax.psum(shard_acc[0].astype(jnp.bfloat16), 'ctx').astype(jnp.float32)  49.3 us
    reduce_scatter x1, waiting for transfers between devices, spread_grads(): lax.psum_scatter(grads[2].astype(jnp.bfloat16), 'fsdp', scatter_dimension...  48.7 us
    ppermute x3, waiting for transfers between devices, collect(): pieces.append(lax.ppermute(pieces[-1], axis, right))  48.3 us
    psum x1, waiting for transfers between devices, body(): lax.psum(jnp.dot(act_b, wd_all, preferred_element_type=jnp.float32).astyp...  47.2 us
  transfers between devices with their start and end apart: 22, of which 17 were waited for; matrix products, arithmetic and copies ran while one was open for 20% of the time, Pallas kernels for 0%

profile of v1, /device:TPU:0, one launch (start us, length us, event | category | flops | bytes accessed | tf_op | source)
XLA Modules:
  0.0 893.6 jit_solution(1812425311172981996)
XLA Ops:
  10.4 42.3 %all-gather.7.cloned.1.call-done = bf16[3,768,384]{2,1,0:T(8,128)(2,1)} async-done(((bf16[3,192,384]{2,1,0:T(8,128)(2,1)}), bf16[3,768,384]{2,1,0:T(8,128)(2,1)}) %all-gather.7.cloned.1.call-update) | async-done | bytes 1769488 | tf_op jit(solution)/shard_map/all_gather | solution.py:42
  70.4 17.5 %all_gather.36 = bf16[384,768]{0,1:T(8,128)(2,1)} all-gather(bf16[384,192]{0,1:T(8,128)(2,1)S(1)} %copy-done.144), channel_id=1, replica_groups=mesh['fsdp'=4,'ctx'=4,'tp'=2] {'fsdp'}, dimensions={1}, use_global_device_ids=true | all-gather | bytes 737280 | tf_op jit(solution)/shard_map/all_gather | solution.py:43
  98.8 17.9 %all-gather.17.cloned.1.call-done = bf16[2,2,512,384]{3,2,1,0:T(8,128)(2,1)} async-done(((bf16[2,2,128,384]{3,2,1,0:T(8,128)(2,1)}), bf16[2,2,512,384]{3,2,1,0:T(8,128)(2,1)}) %all-gather.17.cloned.1.call-update) | async-done | bytes 1572880 | tf_op jit(solution)/shard_map/all_gather | solution.py:134
  119.5 18.9 %all-gather.15.cloned.1.call-done = bf16[2,2,512,384]{3,2,1,0:T(8,128)(2,1)} async-done(((bf16[2,2,128,384]{3,2,1,0:T(8,128)(2,1)}), bf16[2,2,512,384]{3,2,1,0:T(8,128)(2,1)}) %all-gather.15.cloned.1.call-update) | async-done | bytes 1572880 | tf_op jit(solution)/shard_map/all_gather | solution.py:134
  171.1 16.0 %collective-permute-done = bf16[192,1536]{1,0:T(8,128)(2,1)S(1)} collective-permute-done((bf16[192,1536]{1,0:T(8,128)(2,1)}, bf16[192,1536]{1,0:T(8,128)(2,1)S(1)}, u32[]{:S(2)}, u32[]{:S(2)}) %collective-permute-start) | collective-permute-done | bytes 589856 | tf_op jit(solution)/shard_map/ppermute | solution.py:20
  187.9 16.5 %collective-permute-done.1 = bf16[192,1536]{1,0:T(8,128)(2,1)} collective-permute-done((bf16[192,1536]{1,0:T(8,128)(2,1)S(1)}, bf16[192,1536]{1,0:T(8,128)(2,1)}, u32[]{:S(2)}, u32[]{:S(2)}) %collective-permute-start.1) | collective-permute-done | bytes 589856 | tf_op jit(solution)/shard_map/ppermute | solution.py:20
  204.6 15.7 %collective-permute-done.2 = bf16[192,1536]{1,0:T(8,128)(2,1)} collective-permute-done((bf16[192,1536]{1,0:T(8,128)(2,1)}, bf16[192,1536]{1,0:T(8,128)(2,1)}, u32[]{:S(2)}, u32[]{:S(2)}) %collective-permute-start.2) | collective-permute-done | bytes 589856 | tf_op jit(solution)/shard_map/ppermute | solution.py:20
  227.7 28.3 %all-reduce.13.cloned.1.call-done = (f32[256,768]{1,0:T(8,128)}, f32[256,768]{1,0:T(8,128)}, f32[256,768]{1,0:T(8,128)}, f32[256,768]{1,0:T(8,128)}) async-done(((f32[256,768]{1,0:T(8,128)}, f32[256,768]{1,0:T(8,128)}, f32[256,768]{1,0:T(8,128)}, f32[256,768]{1,0:T(8,128)}), (f32[256,768]{1,0:T(8,128)}, f32[256,768]{1,0:T(8,128)}, f32[256,768]{1,0:T(8,128)}, ...) | async-done | bytes 3145744 | tf_op jit(solution)/shard_map/psum | solution.py:142
  261.5 5.8 multiply_convert_fusion.10
  267.4 5.4 multiply_convert_fusion.9
  272.8 5.4 multiply_convert_fusion.8
  278.2 5.4 multiply_convert_fusion.11
  283.6 24.6 %all-gather.11.cloned.1.call-done = bf16[1536,768]{0,1:T(8,128)(2,1)} async-done(((bf16[1536,192]{0,1:T(8,128)(2,1)}), bf16[1536,768]{0,1:T(8,128)(2,1)}) %all-gather.11.cloned.1.call-update) | async-done | bytes 2359312 | tf_op jit(solution)/shard_map/all_gather | solution.py:45
  320.4 47.2 %all-reduce.21.cloned.1.call-done = (bf16[256,768]{1,0:T(8,128)(2,1)}, bf16[256,768]{1,0:T(8,128)(2,1)}, bf16[256,768]{1,0:T(8,128)(2,1)}, bf16[256,768]{1,0:T(8,128)(2,1)}) async-done(((bf16[256,768]{1,0:T(8,128)(2,1)}, bf16[256,768]{1,0:T(8,128)(2,1)}, bf16[256,768]{1,0:T(8,128)(2,1)}, bf16[256,768]{1,0:T(8,128)(2,1)}), (bf16[256,768]{1,0:T(8,128)(2,1)}, bf16[256,768]{1,0:T(8,128)(2,1)}, ...) | async-done | bytes 1572880 | tf_op jit(solution)/shard_map/psum | solution.py:151
  398.4 51.9 %all-reduce.19.cloned.1.call-done = (bf16[256,768]{1,0:T(8,128)(2,1)}, bf16[256,768]{1,0:T(8,128)(2,1)}, bf16[256,768]{1,0:T(8,128)(2,1)}, bf16[256,768]{1,0:T(8,128)(2,1)}) async-done(((bf16[256,768]{1,0:T(8,128)(2,1)}, bf16[256,768]{1,0:T(8,128)(2,1)}, bf16[256,768]{1,0:T(8,128)(2,1)}, bf16[256,768]{1,0:T(8,128)(2,1)}), (bf16[256,768]{1,0:T(8,128)(2,1)}, bf16[256,768]{1,0:T(8,128)(2,1)}, ...) | async-done | bytes 1572880 | tf_op jit(solution)/shard_map/psum | solution.py:169
  567.0 7.0 reduce-scatter.25.cloned.1.call-done
  575.2 30.2 %reduce-scatter.29.cloned.1.call-done = bf16[128,1536]{1,0:T(8,128)(2,1)} async-done(((bf16[512,1536]{1,0:T(8,128)(2,1)}), bf16[128,1536]{1,0:T(8,128)(2,1)}) %reduce-scatter.29.cloned.1.call-update) | async-done | bytes 393232
  654.2 19.4 %all-reduce = (bf16[2,384]{1,0:T(2,128)(2,1)S(1)}, bf16[768]{0:T(1024)(128)(2,1)S(1)}, bf16[768]{0:T(1024)(128)(2,1)S(1)}, bf16[768]{0:T(1024)(128)(2,1)S(1)}, b...) all-reduce(f32[2,384]{1,0:T(2,128)S(1)} %add_add_fusion.15, ...), channel_id=1, replica_groups=mesh['fsdp'=4,'ctx'=4,'tp'=2] {'fsdp'}, use_global_device_ids=true, to_apply=%region_70.71 | all-reduce | flops 6912 | bytes 41472 | tf_op jit(solution)/shard_map/psum | solution.py:224
  673.5 11.0 %all-reduce.2 = (bf16[2,384]{1,0:T(2,128)(2,1)S(1)}, bf16[768]{0:T(1024)(128)(2,1)S(1)}, bf16[768]{0:T(1024)(128)(2,1)S(1)}, bf16[768]{0:T(1024)(128)(2,1)S(1)},...) all-reduce(bf16[2,384]{1,0:T(2,128)(2,1)S(1)} %get-tuple-element.10, ...), channel_id=1, replica_groups=mesh['fsdp'=4,'ctx'=4,'tp'=2] {'ctx'}, use_global_device_ids=true, to_apply=%region_71.72 | all-reduce | flops 6912 | bytes 27648 | tf_op jit(solution)/shard_map/psum | solution.py:242
  690.4 16.5 %reduce-scatter.33.cloned.1.call-done = bf16[192,1152]{1,0:T(8,128)(2,1)} async-done(((bf16[768,1152]{1,0:T(8,128)(2,1)}), bf16[192,1152]{1,0:T(8,128)(2,1)}) %reduce-scatter.33.cloned.1.call-update) | async-done | bytes 442384
  709.6 21.2 %reduce-scatter.19.cloned.1.call-done = bf16[384,192]{0,1:T(8,128)(2,1)} async-done(((bf16[384,768]{0,1:T(8,128)(2,1)}), bf16[384,192]{0,1:T(8,128)(2,1)}) %reduce-scatter.19.cloned.1.call-update) | async-done | bytes 147472 | tf_op jit(solution)/shard_map/reduce_scatter | solution.py:54
  730.9 48.7 %reduce-scatter.21.cloned.1.call-done = bf16[192,1536]{1,0:T(8,128)(2,1)} async-done(((bf16[768,1536]{1,0:T(8,128)(2,1)}), bf16[192,1536]{1,0:T(8,128)(2,1)}) %reduce-scatter.21.cloned.1.call-update) | async-done | bytes 589840 | tf_op jit(solution)/shard_map/reduce_scatter | solution.py:57
  779.5 49.8 %reduce-scatter.23.cloned.1.call-done = bf16[1536,192]{0,1:T(8,128)(2,1)} async-done(((bf16[1536,768]{0,1:T(8,128)(2,1)}), bf16[1536,192]{0,1:T(8,128)(2,1)}) %reduce-scatter.23.cloned.1.call-update) | async-done | bytes 589840 | tf_op jit(solution)/shard_map/reduce_scatter | solution.py:60
  832.1 49.3 %all-reduce.15.cloned.1.call-done = (bf16[3,192,384]{1,2,0:T(8,128)(2,1)}, bf16[384,192]{0,1:T(8,128)(2,1)}, bf16[192,1536]{1,0:T(8,128)(2,1)}, bf16[1536,192]{0,1:T(8,128)(2,1)}) async-done(((bf16[3,192,384]{1,2,0:T(8,128)(2,1)}, bf16[384,192]{0,1:T(8,128)(2,1)}, bf16[192,1536]{1,0:T(8,128)(2,1)}, bf16[1536,192]{0,1:T(8,128)(2,1)}), (bf16[3,192,384]{1,2,0:T(8,128)(2,1)}, bf16[384,192]{0,1:T(8,128)(2,1)}, ...) | async-done | bytes 1769488 | tf_op jit(solution)/shard_map/psum | solution.py:238
  (766 shorter events, 304.4 us)
Async XLA Ops:
  7.2 45.5 %all-gather.7.cloned.1.call-start = ((), (), s32[]{:S(2)}) async-start(), calls=%async_computation.8 | async-start | bytes 2211840 | tf_op jit(solution)/shard_map/all_gather | solution.py:42
  7.9 85.4 %all-gather.9.cloned.1.call-start = ((), (), s32[]{:S(2)}) async-start(), calls=%async_computation.9 | async-start | bytes 1966080 | tf_op jit(solution)/shard_map/all_gather | solution.py:134
  55.6 40.5 %all-gather.13.cloned.1.call-start = ((), (), s32[]{:S(2)}) async-start(), calls=%async_computation.11 | async-start | bytes 1966080 | tf_op jit(solution)/shard_map/all_gather | solution.py:134
  58.7 58.0 %all-gather.17.cloned.1.call-start = ((), (), s32[]{:S(2)}) async-start(), calls=%async_computation.13 | async-start | bytes 1966080 | tf_op jit(solution)/shard_map/all_gather | solution.py:134
  61.9 76.6 %all-gather.15.cloned.1.call-start = ((), (), s32[]{:S(2)}) async-start(), calls=%async_computation.12 | async-start | bytes 1966080 | tf_op jit(solution)/shard_map/all_gather | solution.py:134
  65.1 190.9 %all-reduce.13.cloned.1.call-start = ((), (), s32[]{:S(2)}) async-start(), calls=%async_computation.22 | async-start | bytes 6291456 | tf_op jit(solution)/shard_map/psum | solution.py:142
  169.5 138.7 %all-gather.11.cloned.1.call-start = ((), (), s32[]{:S(2)}) async-start(), calls=%async_computation.10 | async-start | bytes 2949120 | tf_op jit(solution)/shard_map/all_gather | solution.py:45
  169.6 17.5 %collective-permute-start = (bf16[192,1536]{1,0:T(8,128)(2,1)}, bf16[192,1536]{1,0:T(8,128)(2,1)S(1)}, u32[]{:S(2)}, u32[]{:S(2)}) collective-permute-start(bf16[192,1536]{1,0:T(8,128)(2,1)} %param.23), channel_id=1, source_target_pairs={{0,8},{8,16},{16,24},{24,0},{1,9},{9,17},{17,25},{25,1},{2,10},{10... | collective-permute-start | bytes 1769480 | tf_op jit(solution)/shard_map/ppermute | solution.py:20
  187.9 16.5 %collective-permute-start.1 = (bf16[192,1536]{1,0:T(8,128)(2,1)S(1)}, bf16[192,1536]{1,0:T(8,128)(2,1)}, u32[]{:S(2)}, u32[]{:S(2)}) collective-permute-start(bf16[192,1536]{1,0:T(8,128)(2,1)S(1)} %collective-permute-done), channel_id=1, source_target_pairs={{0,8},{8,16},{16,24},{24,0},{1,9},{9,17},{17,25},{25,1},{2,10},{10... | collective-permute-start | bytes 1769480 | tf_op jit(solution)/shard_map/ppermute | solution.py:20
  204.5 15.8 %collective-permute-start.2 = (bf16[192,1536]{1,0:T(8,128)(2,1)}, bf16[192,1536]{1,0:T(8,128)(2,1)}, u32[]{:S(2)}, u32[]{:S(2)}) collective-permute-start(bf16[192,1536]{1,0:T(8,128)(2,1)} %collective-permute-done.1), channel_id=1, source_target_pairs={{0,8},{8,16},{16,24},{24,0},{1,9},{9,17},{17,25},{25,1},{2,10},{10... | collective-permute-start | bytes 1769480 | tf_op jit(solution)/shard_map/ppermute | solution.py:20
  204.5 163.1 %all-reduce.21.cloned.1.call-start = ((), (), s32[]{:S(2)}) async-start(), calls=%async_computation.26 | async-start | bytes 3145728 | tf_op jit(solution)/shard_map/psum | solution.py:151
  316.5 133.8 %all-reduce.19.cloned.1.call-start = ((), (), s32[]{:S(2)}) async-start(), calls=%async_computation.25 | async-start | bytes 3145728 | tf_op jit(solution)/shard_map/psum | solution.py:169
  398.1 166.3 %reduce-scatter.31.cloned.1.call-start = ((), (), s32[]{:S(2)}) async-start(), calls=%async_computation.20 | async-start | bytes 1966080
  484.1 81.6 %reduce-scatter.27.cloned.1.call-start = ((), (), s32[]{:S(2)}) async-start(), calls=%async_computation.18 | async-start | bytes 1966080
  508.7 65.3 %reduce-scatter.25.cloned.1.call-start = ((), (), s32[]{:S(2)}) async-start(), calls=%async_computation.17 | async-start | bytes 1966080
  532.5 72.8 %reduce-scatter.29.cloned.1.call-start = ((), (), s32[]{:S(2)}) async-start(), calls=%async_computation.19 | async-start | bytes 1966080
  552.0 137.4 %all-reduce.17.cloned.1.call-start = ((), (), s32[]{:S(2)}) async-start(), calls=%async_computation.24 | async-start | bytes 3145728 | tf_op jit(solution)/shard_map/psum | solution.py:219
  565.7 51.9 %copy-start.61 = (bf16[2,2,128,384]{3,2,1,0:T(8,128)(2,1)}, bf16[2,2,128,384]{3,2,1,0:T(8,128)(2,1)S(1)}, u32[]{:S(2)}) copy-start(bf16[2,2,128,384]{3,2,1,0:T(8,128)(2,1)S(1)} %copy.161) | copy-start | bytes 1179652
  614.1 92.8 %reduce-scatter.33.cloned.1.call-start = ((), (), s32[]{:S(2)}) async-start(), calls=%async_computation.21 | async-start | bytes 2211840
  625.1 105.8 %reduce-scatter.19.cloned.1.call-start = ((), (), s32[]{:S(2)}) async-start(), calls=%async_computation.14 | async-start | bytes 737280 | tf_op jit(solution)/shard_map/reduce_scatter | solution.py:54
  634.4 145.2 %reduce-scatter.21.cloned.1.call-start = ((), (), s32[]{:S(2)}) async-start(), calls=%async_computation.15 | async-start | bytes 2949120 | tf_op jit(solution)/shard_map/reduce_scatter | solution.py:57
  640.9 188.5 %reduce-scatter.23.cloned.1.call-start = ((), (), s32[]{:S(2)}) async-start(), calls=%async_computation.16 | async-start | bytes 2949120 | tf_op jit(solution)/shard_map/reduce_scatter | solution.py:60
  649.4 232.1 %all-reduce.15.cloned.1.call-start = ((), (), s32[]{:S(2)}) async-start(), calls=%async_computation.23 | async-start | bytes 3833856 | tf_op jit(solution)/shard_map/psum | solution.py:238
  708.4 121.0 %copy-start.142 = (bf16[256,768]{1,0:T(8,128)(2,1)S(1)}, bf16[256,768]{1,0:T(8,128)(2,1)}, u32[]{:S(2)}) copy-start(bf16[256,768]{1,0:T(8,128)(2,1)} %get-tuple-element.126) | copy-start | bytes 1179652
  (233 other events, 1137.2 us)
Sparse Core Ops, SparseCore 0:
  9.6 43.0 all-gather.6
  55.7 18.6 all-gather.8
  76.0 19.6 all-gather.12
  97.1 19.6 all-gather.16
  118.7 19.6 all-gather.14
  169.6 86.3 all-reduce.12
  257.7 50.4 all-gather.10
  316.6 50.8 all-reduce.20
  398.2 52.0 all-reduce.18
  484.3 28.1 reduce-scatter.30
  515.0 28.1 reduce-scatter.26
  545.8 28.1 reduce-scatter.24
  577.1 28.1 reduce-scatter.28
  614.2 52.0 all-reduce.16
  668.5 38.3 reduce-scatter.32
  709.7 21.0 reduce-scatter.18
  733.1 46.3 reduce-scatter.20
  781.8 47.5 reduce-scatter.22
  832.7 48.6 all-reduce.14
